TPU v7x, 32 devices: a whole 2x2x4 slice. The times are simulated.
32 devices in a mesh: grp: 2 (over y), band: 8 (over z, x), filt: 2 (over core).
Axes of the slice: x: 2, y: 2, z: 4, core: 2. Of those that a mesh axis runs over, the one named last changes fastest.
Arguments:
- coeff_maps: bfloat16 [128, 64, 512], P(('grp', 'filt'), 'band'), parts along dimension 0, may hold values from -0.75 to 0.75
- image: bfloat16 [6, 64, 512], P('grp', 'band'), parts along dimension 0, may hold values from -24 to 24
- target: bfloat16 [1024, 2, 3, 64, 64], P(('grp', 'band'), None, None, 'filt'), parts along dimension 0, may hold values from -1.5 to 1.5
- dual_rim: float32 [128, 768], P(('grp', 'filt')), parts along dimension 0, may hold values from -18 to 18, as said below
Outputs:
- dict_spectra: bfloat16 [1024, 2, 3, 64, 64], P(('grp', 'band'), None, None, 'filt'), parts along dimension 0
- dictionary: float32 [128, 768], P(('grp', 'filt')), parts along dimension 0
There are 2 independent parts, one for each index of `grp`. A program takes and returns all parts, laid end to end along the dimension named above; each array names one. Nothing has to cross between parts.
Inputs may be any that keep to these rules, and one draw needn't show every extreme that they name: `dual_rim`: a scaled dual variable on the filters' support.
All inputs are finite; a program needn't handle non-finite values.
Results may differ from a plain program's by a relative error of at most 0.0059.
Values may be sent and summed in bfloat16 or wider, within the bound.
No kernel may reach another device: no remote copies, remote signals or barrier semaphores. Data moves between devices by JAX's collectives and lax.ppermute only.
A program may use at most 128 MiB of HBM per device.

v0:
```python
import math
import jax
import jax.numpy as jnp
from jax import lax
from jax.sharding import PartitionSpec as P

K = 16
penalty = 1.0


def forward_columns(length):
    ramp = jnp.arange(length, dtype=jnp.int32)
    phases = ramp[:, None] * ramp[None, :] % length
    angles = phases.astype(jnp.float32) * (2.0 * math.pi / length)
    factor = 1.0 / math.sqrt(length)
    lookup = jnp.stack([jnp.cos(angles) * factor, -jnp.sin(angles) * factor], axis=2)
    return lookup.reshape(length, 2 * length).astype(jnp.bfloat16)


def forward_rows(length):
    ramp = jnp.arange(length, dtype=jnp.int32)
    phases = ramp[:, None] * ramp[None, :] % length
    angles = phases.astype(jnp.float32) * (2.0 * math.pi / length)
    factor = 1.0 / math.sqrt(length)
    return jnp.stack([jnp.cos(angles) * factor, jnp.sin(angles) * factor], axis=0).astype(
        jnp.bfloat16
    )


def inverse_rows(length, width):
    ramp = jnp.arange(length, dtype=jnp.int32)
    reach = jnp.arange(width, dtype=jnp.int32)
    phases = ramp[:, None] * reach[None, :] % length
    angles = phases.astype(jnp.float32) * (2.0 * math.pi / length)
    factor = 1.0 / math.sqrt(length)
    return jnp.stack([jnp.cos(angles) * factor, jnp.sin(angles) * factor], axis=1)


def inverse_columns(length, total_cols, width):
    freqs = jnp.arange(length, dtype=jnp.int32)
    reach = jnp.arange(width, dtype=jnp.int32)
    phases = freqs[:, None] * reach[None, :] % total_cols
    angles = phases.astype(jnp.float32) * (2.0 * math.pi / total_cols)
    factor = 1.0 / math.sqrt(total_cols)
    return jnp.stack([jnp.cos(angles) * factor, jnp.sin(angles) * factor], axis=1)


def spectra(slab_rows, lookup, freqs, members):
    height = slab_rows.shape[0]
    products = jnp.einsum("hk,tgh->ktg", slab_rows, lookup, preferred_element_type=jnp.float32)
    products = products.reshape(freqs, 2, members, 2, height)
    real_part = products[:, 0, :, 0] + products[:, 1, :, 1]
    imag_part = products[:, 1, :, 0] - products[:, 0, :, 1]
    return (real_part, imag_part)


def body(coeff_maps, image, target, dual_rim):
    filters, band_rows, width_cols = coeff_maps.shape
    channels = image.shape[0]
    band_count = lax.axis_size("band")
    height = band_rows * band_count
    per_band = width_cols // band_count
    col_lookup = forward_columns(width_cols)
    row_lookup = forward_rows(height)
    col_maps = jnp.einsum("mrn,nk->rkm", coeff_maps, col_lookup, preferred_element_type=jnp.float32)
    col_maps = col_maps.astype(jnp.bfloat16).reshape(band_rows, 2 * width_cols * filters)
    col_image = jnp.einsum("crn,nk->rkc", image, col_lookup, preferred_element_type=jnp.float32)
    col_image = col_image.astype(jnp.bfloat16).reshape(band_rows, 2 * width_cols * channels)
    got_maps, got_image = (
        lax.all_to_all(col_maps, "band", split_axis=1, concat_axis=0, tiled=True),
        lax.all_to_all(col_image, "band", split_axis=1, concat_axis=0, tiled=True),
    )
    x_re, x_im = spectra(got_maps, row_lookup, per_band, filters)
    s_re, s_im = spectra(got_image, row_lookup, per_band, channels)
    v_full = target.astype(jnp.float32)
    v_re = v_full[:, 0]
    v_im = v_full[:, 1]
    energy = jnp.sum(x_re * x_re + x_im * x_im, axis=1)
    cross_re = jnp.sum(x_re[:, None] * v_re - x_im[:, None] * v_im, axis=2)
    cross_im = jnp.sum(x_re[:, None] * v_im + x_im[:, None] * v_re, axis=2)
    energy, cross_re, cross_im = (
        lax.psum(energy.astype(jnp.bfloat16), "filt").astype(jnp.float32),
        lax.psum(cross_re.astype(jnp.bfloat16), "filt").astype(jnp.float32),
        lax.psum(cross_im.astype(jnp.bfloat16), "filt").astype(jnp.float32),
    )
    denom = penalty + energy[:, None, :]
    coef_re = (s_re - cross_re) / denom
    coef_im = (s_im - cross_im) / denom
    dict_real = v_re + x_re[:, None] * coef_re[:, :, None] + x_im[:, None] * coef_im[:, :, None]
    dict_imag = v_im + x_re[:, None] * coef_im[:, :, None] - x_im[:, None] * coef_re[:, :, None]
    dict_full = jnp.stack([dict_real, dict_imag], axis=1)
    dict_spectra = dict_full.astype(jnp.bfloat16)
    rim_lookup = inverse_rows(height, K)
    folded = jnp.einsum("qpcmg,gty->qpcmty", dict_full, rim_lookup, precision=lax.Precision.HIGHEST)
    rim_real = folded[:, 0, :, :, 0] - folded[:, 1, :, :, 1]
    rim_imag = folded[:, 0, :, :, 1] + folded[:, 1, :, :, 0]
    start_sum = jnp.zeros((filters, channels, K, K), jnp.float32)
    running = start_sum
    pieces = (
        lax.all_gather(rim_real.astype(jnp.bfloat16), "band", axis=0, tiled=True).astype(
            jnp.float32
        ),
        lax.all_gather(rim_imag.astype(jnp.bfloat16), "band", axis=0, tiled=True).astype(
            jnp.float32
        ),
    )
    length = pieces[0].shape[0]
    lookup = inverse_columns(length, width_cols, K)
    running = running + jnp.einsum(
        "qcmy,qx->mcyx", pieces[0], lookup[:, 0], precision=lax.Precision.HIGHEST
    )
    spatial = running - jnp.einsum(
        "qcmy,qx->mcyx", pieces[1], lookup[:, 1], precision=lax.Precision.HIGHEST
    )
    joined = spatial.reshape(filters, channels * K * K) + dual_rim
    spread = jnp.sqrt(jnp.mean(joined * joined, axis=1, keepdims=True))
    dictionary = joined / jnp.maximum(spread, 1.0)
    return (dict_spectra, dictionary)


def solution(mesh):
    placed = (
        P(("grp", "filt"), "band", None),
        P("grp", "band", None),
        P(("grp", "band"), None, None, "filt", None),
        P(("grp", "filt"), None),
    )
    return jax.shard_map(
        body,
        mesh=mesh,
        in_specs=placed,
        out_specs=(P(("grp", "band"), None, None, "filt", None), P(("grp", "filt"), None)),
        check_vma=False,
    )
```

profile of v0, /device:TPU:0, one launch (start us, length us, event | category | flops | bytes accessed | tf_op | source)
XLA Modules:
  0.0 297.8 jit_solution(11534772521772797656)
XLA Ops:
  7.2 4.4 %multiply_convert_fusion = (bf16[512,512,1]{1,0,2:T(8,128)(2,1)S(1)}, bf16[512,512,1]{1,0,2:T(8,128)(2,1)S(1)}) fusion(), kind=kLoop, calls=%fused_computation.42 | loop fusion | flops 4980736 | bytes 1048576 | tf_op jit(solution)/shard_map/convert.3
  11.6 0.1 pad_maximum_fusion.2
  11.7 1.0 copy.59
  12.7 0.4 convert_element_type.110
  13.1 0.4 fusion.15
  13.5 0.7 copy.69
  14.2 0.6 all_to_all.32
  14.9 0.9 copy.70
  15.7 7.3 %all-to-all-start.1 = ((bf16[8,8,384]{2,0,1:T(8,128)(2,1)}), bf16[8,8,384]{2,0,1:T(8,128)(2,1)S(1)}, u32[]{:S(2)}, u32[]{:S(2)}) async-start(bf16[8,8,384]{2,0,1:T(8,128)(2,1)} %copy.70), calls=%async_computation.1 | async-start | bytes 98304 | tf_op jit(solution)/shard_map/all_to_all | solution.py:71
  23.0 0.5 fusion.11
  23.5 1.0 copy.62
  24.5 2.3 all_to_all.28
  26.8 1.1 copy.63
  27.9 1.9 all-to-all-done.1
  29.8 4.1 %all-to-all-start = ((bf16[8,8,4096]{2,0,1:T(8,128)(2,1)}), bf16[8,8,4096]{2,0,1:T(8,128)(2,1)S(1)}, u32[]{:S(2)}, u32[]{:S(2)}) async-start(bf16[8,8,4096]{2,0,1:T(8,128)(2,1)} %copy.63), calls=%async_computation | async-start | bytes 1048576 | tf_op jit(solution)/shard_map/all_to_all | solution.py:70
  33.9 0.0 all-gather.7.cloned.1.call-start
  33.9 0.1 sine_multiply_fusion
  34.0 0.2 multiply_convert_fusion.2
  34.1 6.4 %copy_convert_fusion = f32[64,2,3,32,64]{4,0,3,2,1:T(8,128)} fusion(bf16[64,2,3,32,64]{4,3,2,1,0:T(8,128)(2,1)} %param.6), kind=kLoop, calls=%fused_computation.12 | loop fusion | flops 786432 | bytes 4718592 | tf_op jit(solution)/shard_map/convert_element_type | solution.py:75
  40.5 0.1 copy.71
  40.6 0.1 dot_general.35
  40.7 0.2 fusion.39
  40.9 6.9 %all-to-all-done = bf16[8,8,4096]{2,0,1:T(8,128)(2,1)S(1)} async-done(((bf16[8,8,4096]{2,0,1:T(8,128)(2,1)}), bf16[8,8,4096]{2,0,1:T(8,128)(2,1)S(1)}, u32[]{:S(2)}, u32[]{:S(2)}) %all-to-all-start) | async-done | bytes 524320 | tf_op jit(solution)/shard_map/all_to_all | solution.py:70
  47.9 0.5 copy.64
  48.4 0.9 fusion.22
  49.2 0.7 add_reduce_fusion
  49.9 0.6 slice-done
  50.5 1.4 slice-done.1
  51.9 1.1 fusion.4
  53.0 3.9 %all-reduce = (bf16[64,3,64]{2,0,1:T(8,128)(2,1)S(1)}, bf16[64,64]{1,0:T(8,128)(2,1)S(1)}, bf16[64,3,64]{2,0,1:T(8,128)(2,1)S(1)}) all-reduce(bf16[64,3,64]{2,0,1:T(8,128)(2,1)S(1)} %get-tuple-element.11, bf16[64,64]{1,0:T(8,128)(2,1)S(1)} %get-tuple-element.17, ...), channel_id=1, replica_groups=mesh['grp'=2,'band'=8,'filt'=2] {'filt'}, use_global_device_ids=true, to_apply=%region_5.6 | all-reduce | flops 28672 | bytes 114688 | tf_op jit(solution)/shard_map/psum | solution.py:84
  57.0 4.5 %multiply_add_fusion = (f32[64,1,3,32,64]{4,0,3,2,1:T(8,128)S(1)}, f32[64,1,3,32,64]{4,0,3,2,1:T(8,128)S(1)}) fusion(f32[64,2,3,32,64]{4,0,3,2,1:T(8,128)} %copy_convert_fusion, f32[64,3,64]{2,0,1:T(8,128)S(1)} %get-tuple-element.25, f32[64,32,64]{2,0,1:T(8,128)} %copy-done.3, f32[64,3,64]{2,0,1:T(8,128)S(1)} %get-tuple-element.24, f32[64,32,64]{2,0,1:T(8,128)} %copy-done.2), kind=kLoop, calls=%fused_computation.14 | loop fusion | flops 3145728 | bytes 7438336 | tf_op jit(solution)/shard_map/add | solution.py:89
  61.5 17.3 %fusion = f32[64,2,3,32,2,16]{0,5,4,3,2,1:T(8,128)S(1)} fusion(f32[64,1,3,32,64]{4,0,3,2,1:T(8,128)S(1)} %get-tuple-element.21, f32[64,1,3,32,64]{4,0,3,2,1:T(8,128)S(1)} %get-tuple-element.20, f32[64,1,16]{0,2,1:T(8,128)S(1)} %get-tuple-element.30, f32[64,1,16]{0,2,1:T(8,128)S(1)} %get-tuple-element.31), kind=kOutput, calls=%fused_computation.1 | convolution fusion | flops 302778368 | bytes 4726784 | tf_op jit(solution)/shard_map/qpcmg,gty->qpcmty/dot_general | solution.py:94
  78.9 1.1 fusion.30
  80.0 2.7 copy.77
  82.7 0.0 all-gather.7.cloned.1.call-update
  82.7 0.3 all-gather.5.cloned.1.call-start
  83.0 2.7 copy.75
  85.7 2.4 fusion.2
  88.1 3.7 %copy.80 = bf16[64,2,3,32,64]{4,3,2,1,0:T(8,128)(2,1)} copy(bf16[64,2,3,32,64]{4,0,3,2,1:T(8,128)(2,1)S(1)} %fusion.2) | data formatting | bytes 3145728
  91.7 89.3 %all-gather.7.cloned.1.call-done = bf16[512,1,3,32,1,16]{3,5,4,2,1,0:T(8,128)(2,1)} async-done(((bf16[64,1,3,32,1,16]{3,5,4,2,1,0:T(8,128)(2,1)}), bf16[512,1,3,32,1,16]{3,5,4,2,1,0:T(8,128)(2,1)}) %all-gather.7.cloned.1.call-update) | async-done | bytes 1572880 | tf_op jit(solution)/shard_map/all_gather | solution.py:103
  181.0 6.4 %copy.78 = bf16[512,1,3,32,1,16]{0,3,5,2,4,1:T(8,128)(2,1)S(1)} copy(bf16[512,1,3,32,1,16]{3,5,4,2,1,0:T(8,128)(2,1)} %all-gather.7.cloned.1.call-done) | data formatting | bytes 3145728 | tf_op jit(solution)/shard_map/all_gather | solution.py:103
  187.4 3.2 %fusion.7 = f32[16,3,32,16]{2,0,3,1:T(8,128)S(1)} fusion(bf16[512,1,3,32,1,16]{0,3,5,2,4,1:T(8,128)(2,1)S(1)} %copy.78), kind=kOutput, calls=%fused_computation.15 | convolution fusion | flops 151117824 | bytes 1671168 | tf_op jit(solution)/shard_map/qcmy,qx->mcyx/dot_general | solution.py:112
  190.5 89.9 %all-gather.5.cloned.1.call-done = bf16[512,1,3,32,1,16]{3,5,4,2,1,0:T(8,128)(2,1)} async-done(((bf16[64,1,3,32,1,16]{3,5,4,2,1,0:T(8,128)(2,1)}), bf16[512,1,3,32,1,16]{3,5,4,2,1,0:T(8,128)(2,1)}) %all-gather.5.cloned.1.call-update) | async-done | bytes 1572880 | tf_op jit(solution)/shard_map/all_gather | solution.py:100
  280.4 6.4 %copy.76 = bf16[512,1,3,32,1,16]{0,3,5,2,4,1:T(8,128)(2,1)S(1)} copy(bf16[512,1,3,32,1,16]{3,5,4,2,1,0:T(8,128)(2,1)} %all-gather.5.cloned.1.call-done) | data formatting | bytes 3145728 | tf_op jit(solution)/shard_map/all_gather | solution.py:100
  286.8 3.2 %fusion.12 = f32[16,3,32,16]{2,0,3,1:T(8,128)S(1)} fusion(f32[16,3,32,16]{2,0,3,1:T(8,128)S(1)} %fusion.7, bf16[512,1,3,32,1,16]{0,3,5,2,4,1:T(8,128)(2,1)S(1)} %copy.76), kind=kOutput, calls=%fused_computation.24 | convolution fusion | flops 151142400 | bytes 1769472 | tf_op jit(solution)/shard_map/qcmy,qx->mcyx/dot_general | solution.py:109
  290.0 0.2 copy.79
  290.1 0.1 multiply_reduce_fusion
  290.3 0.7 broadcast_divide_fusion
  (19 shorter events, 0.1 us)
Async XLA Ops:
  7.2 15.8 %copy-start = (bf16[32,8,512]{2,1,0:T(8,128)(2,1)S(1)}, bf16[32,8,512]{2,1,0:T(8,128)(2,1)}, u32[]{:S(2)}) copy-start(bf16[32,8,512]{2,1,0:T(8,128)(2,1)} %param.4) | copy-start | bytes 786436
  11.6 1.6 copy-start.5
  15.7 14.0 %all-to-all-start.1 = ((bf16[8,8,384]{2,0,1:T(8,128)(2,1)}), bf16[8,8,384]{2,0,1:T(8,128)(2,1)S(1)}, u32[]{:S(2)}, u32[]{:S(2)}) async-start(bf16[8,8,384]{2,0,1:T(8,128)(2,1)} %copy.70), calls=%async_computation.1 | async-start | bytes 98304 | tf_op jit(solution)/shard_map/all_to_all | solution.py:71
  29.8 18.1 %all-to-all-start = ((bf16[8,8,4096]{2,0,1:T(8,128)(2,1)}), bf16[8,8,4096]{2,0,1:T(8,128)(2,1)S(1)}, u32[]{:S(2)}, u32[]{:S(2)}) async-start(bf16[8,8,4096]{2,0,1:T(8,128)(2,1)} %copy.63), calls=%async_computation | async-start | bytes 1048576 | tf_op jit(solution)/shard_map/all_to_all | solution.py:70
  33.9 147.1 %all-gather.7.cloned.1.call-start = ((), (), s32[]{:S(2)}) async-start(), calls=%async_computation.3 | async-start | bytes 7077888 | tf_op jit(solution)/shard_map/all_gather | solution.py:103
  48.3 2.2 slice-start
  48.3 3.6 %slice-start.1 = ((s8[6291456]{0:T(1024)(128)(4,1)}), s8[2097152]{0:T(1024)(128)(4,1)S(1)}, s32[]{:S(2)}) async-start(s8[6291456]{0:T(1024)(128)(4,1)} %bitcast.128), calls=%async_computation.5 | async-start | bytes 4194304
  49.9 3.1 %copy-start.2 = (f32[64,32,64]{2,0,1:T(8,128)}, f32[64,32,64]{2,0,1:T(8,128)S(1)}, u32[]{:S(2)}) copy-start(f32[64,32,64]{2,0,1:T(8,128)S(1)} %get-tuple-element.18) | copy-start | bytes 1572868
  49.9 3.1 %copy-start.3 = (f32[64,32,64]{2,0,1:T(8,128)}, f32[64,32,64]{2,0,1:T(8,128)S(1)}, u32[]{:S(2)}) copy-start(f32[64,32,64]{2,0,1:T(8,128)S(1)} %get-tuple-element.19) | copy-start | bytes 1572868
  61.5 17.4 %copy-start.1 = (f32[64,1,3,32,64]{4,0,3,2,1:T(8,128)}, f32[64,1,3,32,64]{4,0,3,2,1:T(8,128)S(1)}, u32[]{:S(2)}) copy-start(f32[64,1,3,32,64]{4,0,3,2,1:T(8,128)S(1)} %get-tuple-element.21) | copy-start | bytes 4718596
  82.7 197.7 %all-gather.5.cloned.1.call-start = ((), (), s32[]{:S(2)}) async-start(), calls=%async_computation.2 | async-start | bytes 7077888 | tf_op jit(solution)/shard_map/all_gather | solution.py:100
  190.5 99.6 %copy-start.4 = (f32[32,768]{1,0:T(8,128)S(1)}, f32[32,768]{1,0:T(8,128)}, u32[]{:S(2)}) copy-start(f32[32,768]{1,0:T(8,128)} %param.7) | copy-start | bytes 294916
Sparse Core Ops, SparseCore 0:
  82.9 98.1 all-gather.6
  183.2 97.1 all-gather.4
where the time goes:
time: 298 us
  waiting for transfers between devices  188 us (63%)
  local copies, waits for them, and re-layouts  32.7 us (11%)
  matrix products  25.6 us (9%)
  other arithmetic  21.7 us (7%)
  between operations  14.3 us (5%)
  starting transfers between devices  11.6 us (4%)
  blocking collectives  3.9 us (1%)
    all_gather x1, waiting for transfers between devices, body(): lax.all_gather(rim_real.astype(jnp.bfloat16), 'band', axis=0, tiled=True)  89.9 us
    all_gather x1, waiting for transfers between devices, body(): lax.all_gather(rim_imag.astype(jnp.bfloat16), 'band', axis=0, tiled=True)  89.3 us
    dot_general x1, matrix products, body(): jnp.einsum('qpcmg,gty->qpcmty', dict_full, rim_lookup, precision=lax.Prec...  17.3 us
    all_to_all x1, starting transfers between devices, body(): lax.all_to_all(col_image, 'band', split_axis=1, concat_axis=0, tiled=True)  7.25 us
    all_to_all x1, waiting for transfers between devices, body(): lax.all_to_all(col_maps, 'band', split_axis=1, concat_axis=0, tiled=True)  6.91 us
    convert_element_type x1, other arithmetic, body(): v_full = target.astype(jnp.float32)  6.37 us
    all_gather x1, local copies, waits for them, and re-layouts, body(): lax.all_gather(rim_imag.astype(jnp.bfloat16), 'band', axis=0, tiled=True)  6.36 us
    all_gather x1, local copies, waits for them, and re-layouts, body(): lax.all_gather(rim_real.astype(jnp.bfloat16), 'band', axis=0, tiled=True)  6.36 us
  transfers between devices with their start and end apart: 4, of which 4 were waited for; matrix products, arithmetic and copies ran while one was open for 9% of the time, Pallas kernels for 0%

commit v1 on v0

--- a/solution.py
+++ b/solution.py
@@ -6,6 +6,29 @@
 
 K = 16
 penalty = 1.0
+
+
+def split_up(x, dim, size):
+    before, after = (x.shape[:dim], x.shape[dim + 1 :])
+    return jnp.moveaxis(x.reshape(*before, size, -1, *after), dim, 0)
+
+
+def in_order(tiles, dim):
+    tiles = jnp.moveaxis(tiles, 0, dim)
+    lengths = tiles.shape
+    return tiles.reshape(*lengths[:dim], lengths[dim] * lengths[dim + 1], *lengths[dim + 2 :])
+
+
+def rotated_exchange(x, axis, split_dim, concat_dim):
+    size, index = (lax.axis_size(axis), lax.axis_index(axis))
+    blocks = split_up(x, split_dim, size)
+    out = blocks
+    for step in range(1, size):
+        target, source = ((index + step) % size, (index - step) % size)
+        sent = lax.dynamic_index_in_dim(blocks, target, 0)
+        theirs = lax.ppermute(sent, axis, [(i, (i + step) % size) for i in range(size)])
+        out = lax.dynamic_update_slice_in_dim(out, theirs, source, axis=0)
+    return in_order(out, concat_dim)
 
 
 def forward_columns(length):
@@ -67,7 +90,7 @@
     col_image = jnp.einsum("crn,nk->rkc", image, col_lookup, preferred_element_type=jnp.float32)
     col_image = col_image.astype(jnp.bfloat16).reshape(band_rows, 2 * width_cols * channels)
     got_maps, got_image = (
-        lax.all_to_all(col_maps, "band", split_axis=1, concat_axis=0, tiled=True),
+        rotated_exchange(col_maps, "band", 1, 0),
         lax.all_to_all(col_image, "band", split_axis=1, concat_axis=0, tiled=True),
     )
     x_re, x_im = spectra(got_maps, row_lookup, per_band, filters)

time: 298 us -> 315 us (1.057)
  local copies, waits for them, and re-layouts: 32.7 us -> 49 us
  waiting for transfers between devices: 188 us -> 178 us
  starting transfers between devices: 11.6 us -> 19.7 us
    ppermute x0 -> x7, starting transfers between devices: none -> 16.1 us  [rotated_exchange(): lax.ppermute(sent, axis, [(i, (i + step) % size) for i in range(size)])]
    dynamic_update_slice x0 -> x8, local copies, waits for them, and re-layouts: none -> 15.2 us  [rotated_exchange(): out = lax.dynamic_update_slice_in_dim(out, theirs, source, axis=0)]
    all_to_all x1 -> x0, waiting for transfers between devices: 6.91 us -> none  [body(): lax.all_to_all(col_maps, 'band', split_axis=1, concat_axis=0, tiled=True)]
    all_to_all x1 -> x0, starting transfers between devices: 4.1 us -> none  [body(): lax.all_to_all(col_maps, 'band', split_axis=1, concat_axis=0, tiled=True)]
    all_to_all x1, starting transfers between devices: 7.25 us -> 3.35 us  [body(): lax.all_to_all(col_image, 'band', split_axis=1, concat_axis=0, tiled=True)]
    all_to_all x2 -> x0, local copies, waits for them, and re-layouts: 3.35 us -> none  [body(): lax.all_to_all(col_maps, 'band', split_axis=1, concat_axis=0, tiled=True)]
  transfers between devices with their start and end apart: 4 -> 10, of which waited for: 4 -> 2; matrix products, arithmetic and copies ran while one was open for 9% -> 15% of each run, Pallas kernels for 0% -> 0%
where the time goes in v1:
time: 315 us; the launch traced here: 314 us
  waiting for transfers between devices  178 us (57%)
  local copies, waits for them, and re-layouts  49 us (16%)
  matrix products  26.9 us (9%)
  other arithmetic  21.7 us (7%)
  starting transfers between devices  19.7 us (6%)
  between operations  14.7 us (5%)
  blocking collectives  3.72 us (1%)
    all_gather x1, waiting for transfers between devices, body(): lax.all_gather(rim_real.astype(jnp.bfloat16), 'band', axis=0, tiled=True)  89.9 us
    all_gather x1, waiting for transfers between devices, body(): lax.all_gather(rim_imag.astype(jnp.bfloat16), 'band', axis=0, tiled=True)  88.4 us
    dot_general x1, matrix products, body(): jnp.einsum('qpcmg,gty->qpcmty', dict_full, rim_lookup, precision=lax.Prec...  17.3 us
    ppermute x7, starting transfers between devices, rotated_exchange(): lax.ppermute(sent, axis, [(i, (i + step) % size) for i in range(size)])  16.1 us
    dynamic_update_slice x8, local copies, waits for them, and re-layouts, rotated_exchange(): out = lax.dynamic_update_slice_in_dim(out, theirs, source, axis=0)  15.2 us
    unnamed x17, local copies, waits for them, and re-layouts  6.73 us
    convert_element_type x1, other arithmetic, body(): v_full = target.astype(jnp.float32)  6.38 us
    all_gather x1, local copies, waits for them, and re-layouts, body(): lax.all_gather(rim_imag.astype(jnp.bfloat16), 'band', axis=0, tiled=True)  6.36 us
  transfers between devices with their start and end apart: 10, of which 2 were waited for; matrix products, arithmetic and copies ran while one was open for 15% of the time, Pallas kernels for 0%

profile of v1, /device:TPU:0, one launch (start us, length us, event | category | flops | bytes accessed | tf_op | source)
XLA Modules:
  0.0 313.9 jit_solution(11351707331705280978)
XLA Ops:
  7.3 4.4 %multiply_convert_fusion = (bf16[512,512,1]{1,0,2:T(8,128)(2,1)S(1)}, bf16[512,512,1]{1,0,2:T(8,128)(2,1)S(1)}) fusion(), kind=kLoop, calls=%fused_computation.42 | loop fusion | flops 4980736 | bytes 1048576 | tf_op jit(solution)/shard_map/convert.3
  11.8 1.0 copy.59
  13.2 1.0 copy-done.4
  14.2 0.5 fusion.11
  14.7 1.0 copy.62
  15.7 2.3 reshape_reshape.3
  18.0 1.2 dynamic-slice_bitcast_fusion
  19.2 3.0 collective-permute-start
  22.2 1.6 collective-permute-start.1
  23.8 2.6 collective-permute-start.2
  26.3 1.2 collective-permute-start.3
  27.6 2.6 collective-permute-start.4
  30.2 1.6 fusion.15
  31.8 0.7 copy.69
  32.5 0.6 all_to_all.14
  33.1 0.9 copy.70
  34.0 3.3 %all-to-all-start = ((bf16[8,8,384]{2,0,1:T(8,128)(2,1)}), bf16[8,8,384]{2,0,1:T(8,128)(2,1)S(1)}, u32[]{:S(2)}, u32[]{:S(2)}) async-start(bf16[8,8,384]{2,0,1:T(8,128)(2,1)} %copy.70), calls=%async_computation | async-start | bytes 98304 | tf_op jit(solution)/shard_map/all_to_all | solution.py:94
  37.5 6.4 %copy_convert_fusion = f32[64,2,3,32,64]{4,0,3,2,1:T(8,128)} fusion(bf16[64,2,3,32,64]{4,3,2,1,0:T(8,128)(2,1)} %param.6), kind=kLoop, calls=%fused_computation.12 | loop fusion | flops 786432 | bytes 4718592 | tf_op jit(solution)/shard_map/convert_element_type | solution.py:98
  44.1 3.6 %collective-permute-start.5 = (bf16[1,8,4096]{2,0,1:T(2,128)(2,1)S(1)}, bf16[1,8,4096]{2,0,1:T(2,128)(2,1)S(1)}, u32[]{:S(2)}, u32[]{:S(2)}) collective-permute-start(bf16[1,8,4096]{2,0,1:T(2,128)(2,1)S(1)} %get-tuple-element.25), channel_id=1, source_target_pairs={{0,12},{2,14},{4,0},{6,2},{8,4},{10,6},{12,8},{14,10},{1,13},{3,15... | collective-permute-start | bytes 196616 | tf_op jit(solution)/shard_map/ppermute | solution.py:29
  47.7 1.5 collective-permute-start.6
  49.2 2.5 dynamic_update_slice.21
  51.7 2.5 dynamic_update_slice.22
  54.2 2.5 dynamic_update_slice.23
  56.7 2.5 dynamic_update_slice.24
  59.2 2.5 dynamic_update_slice.25
  61.7 1.3 dynamic_update_slice.26
  63.0 1.3 dynamic_update_slice.27
  64.6 0.5 copy.64
  65.1 0.9 fusion.22
  66.0 0.7 add_reduce_fusion
  66.6 0.6 slice-done
  67.3 1.4 slice-done.1
  68.7 1.1 fusion.4
  69.8 3.7 %all-reduce = (bf16[64,3,64]{2,0,1:T(8,128)(2,1)S(1)}, bf16[64,64]{1,0:T(8,128)(2,1)S(1)}, bf16[64,3,64]{2,0,1:T(8,128)(2,1)S(1)}) all-reduce(bf16[64,3,64]{2,0,1:T(8,128)(2,1)S(1)} %get-tuple-element.11, bf16[64,64]{1,0:T(8,128)(2,1)S(1)} %get-tuple-element.17, ...), channel_id=1, replica_groups=mesh['grp'=2,'band'=8,'filt'=2] {'filt'}, use_global_device_ids=true, to_apply=%region_5.6 | all-reduce | flops 28672 | bytes 114688 | tf_op jit(solution)/shard_map/psum | solution.py:107
  74.0 4.5 %multiply_add_fusion = (f32[64,1,3,32,64]{4,0,3,2,1:T(8,128)S(1)}, f32[64,1,3,32,64]{4,0,3,2,1:T(8,128)S(1)}) fusion(f32[64,2,3,32,64]{4,0,3,2,1:T(8,128)} %copy_convert_fusion, f32[64,3,64]{2,0,1:T(8,128)S(1)} %get-tuple-element.32, f32[64,32,64]{2,0,1:T(8,128)} %copy-done.3, f32[64,3,64]{2,0,1:T(8,128)S(1)} %get-tuple-element.31, f32[64,32,64]{2,0,1:T(8,128)} %copy-done.2), kind=kLoop, calls=%fused_computation.14 | loop fusion | flops 3145728 | bytes 7438336 | tf_op jit(solution)/shard_map/add | solution.py:112
  78.5 17.3 %fusion = f32[64,2,3,32,2,16]{0,5,4,3,2,1:T(8,128)S(1)} fusion(f32[64,1,3,32,64]{4,0,3,2,1:T(8,128)S(1)} %get-tuple-element.21, f32[64,1,3,32,64]{4,0,3,2,1:T(8,128)S(1)} %get-tuple-element.20, f32[64,1,16]{0,2,1:T(8,128)S(1)} %get-tuple-element.37, f32[64,1,16]{0,2,1:T(8,128)S(1)} %get-tuple-element.38), kind=kOutput, calls=%fused_computation.1 | convolution fusion | flops 302778368 | bytes 4726784 | tf_op jit(solution)/shard_map/qpcmg,gty->qpcmty/dot_general | solution.py:117
  95.9 1.1 fusion.30
  97.0 2.7 copy.77
  100.0 2.7 copy.75
  102.7 2.4 fusion.2
  105.0 3.7 %copy.80 = bf16[64,2,3,32,64]{4,3,2,1,0:T(8,128)(2,1)} copy(bf16[64,2,3,32,64]{4,0,3,2,1:T(8,128)(2,1)S(1)} %fusion.2) | data formatting | bytes 3145728
  108.7 88.4 %all-gather.7.cloned.1.call-done = bf16[512,1,3,32,1,16]{3,5,4,2,1,0:T(8,128)(2,1)} async-done(((bf16[64,1,3,32,1,16]{3,5,4,2,1,0:T(8,128)(2,1)}), bf16[512,1,3,32,1,16]{3,5,4,2,1,0:T(8,128)(2,1)}) %all-gather.7.cloned.1.call-update) | async-done | bytes 1572880 | tf_op jit(solution)/shard_map/all_gather | solution.py:126
  197.1 6.4 %copy.78 = bf16[512,1,3,32,1,16]{0,3,5,2,4,1:T(8,128)(2,1)S(1)} copy(bf16[512,1,3,32,1,16]{3,5,4,2,1,0:T(8,128)(2,1)} %all-gather.7.cloned.1.call-done) | data formatting | bytes 3145728 | tf_op jit(solution)/shard_map/all_gather | solution.py:126
  203.5 3.2 %fusion.7 = f32[16,3,32,16]{2,0,3,1:T(8,128)S(1)} fusion(bf16[512,1,3,32,1,16]{0,3,5,2,4,1:T(8,128)(2,1)S(1)} %copy.78), kind=kOutput, calls=%fused_computation.15 | convolution fusion | flops 151117824 | bytes 1671168 | tf_op jit(solution)/shard_map/qcmy,qx->mcyx/dot_general | solution.py:135
  206.6 89.9 %all-gather.5.cloned.1.call-done = bf16[512,1,3,32,1,16]{3,5,4,2,1,0:T(8,128)(2,1)} async-done(((bf16[64,1,3,32,1,16]{3,5,4,2,1,0:T(8,128)(2,1)}), bf16[512,1,3,32,1,16]{3,5,4,2,1,0:T(8,128)(2,1)}) %all-gather.5.cloned.1.call-update) | async-done | bytes 1572880 | tf_op jit(solution)/shard_map/all_gather | solution.py:123
  296.5 6.4 %copy.76 = bf16[512,1,3,32,1,16]{0,3,5,2,4,1:T(8,128)(2,1)S(1)} copy(bf16[512,1,3,32,1,16]{3,5,4,2,1,0:T(8,128)(2,1)} %all-gather.5.cloned.1.call-done) | data formatting | bytes 3145728 | tf_op jit(solution)/shard_map/all_gather | solution.py:123
  302.9 3.2 %fusion.12 = f32[16,3,32,16]{2,0,3,1:T(8,128)S(1)} fusion(f32[16,3,32,16]{2,0,3,1:T(8,128)S(1)} %fusion.7, bf16[512,1,3,32,1,16]{0,3,5,2,4,1:T(8,128)(2,1)S(1)} %copy.76), kind=kOutput, calls=%fused_computation.24 | convolution fusion | flops 151142400 | bytes 1769472 | tf_op jit(solution)/shard_map/qcmy,qx->mcyx/dot_general | solution.py:132
  306.4 0.7 broadcast_divide_fusion
  (39 shorter events, 2.2 us)
Async XLA Ops:
  7.2 7.0 %copy-start = (bf16[32,8,512]{2,1,0:T(8,128)(2,1)S(1)}, bf16[32,8,512]{2,1,0:T(8,128)(2,1)}, u32[]{:S(2)}) copy-start(bf16[32,8,512]{2,1,0:T(8,128)(2,1)} %param.4) | copy-start | bytes 786436
  13.2 1.0 copy-start.4
  19.2 24.9 %collective-permute-start = (bf16[1,8,4096]{2,0,1:T(2,128)(2,1)S(1)}, bf16[1,8,4096]{2,0,1:T(2,128)(2,1)}, u32[]{:S(2)}, u32[]{:S(2)}) collective-permute-start(bf16[1,8,4096]{2,0,1:T(2,128)(2,1)S(1)} %get-tuple-element.30), channel_id=1, source_target_pairs={{0,2},{2,4},{4,6},{6,8},{8,10},{10,12},{12,14},{14,0},{1,3},{3,5},... | collective-permute-start | bytes 196616 | tf_op jit(solution)/shard_map/ppermute | solution.py:29
  22.2 25.5 %collective-permute-start.1 = (bf16[1,8,4096]{2,0,1:T(2,128)(2,1)S(1)}, bf16[1,8,4096]{2,0,1:T(2,128)(2,1)}, u32[]{:S(2)}, u32[]{:S(2)}) collective-permute-start(bf16[1,8,4096]{2,0,1:T(2,128)(2,1)S(1)} %get-tuple-element.29), channel_id=1, source_target_pairs={{0,4},{2,6},{4,8},{6,10},{8,12},{10,14},{12,0},{14,2},{1,5},{3,7},... | collective-permute-start | bytes 196616 | tf_op jit(solution)/shard_map/ppermute | solution.py:29
  23.8 30.4 %collective-permute-start.2 = (bf16[1,8,4096]{2,0,1:T(2,128)(2,1)S(1)}, bf16[1,8,4096]{2,0,1:T(2,128)(2,1)}, u32[]{:S(2)}, u32[]{:S(2)}) collective-permute-start(bf16[1,8,4096]{2,0,1:T(2,128)(2,1)S(1)} %get-tuple-element.28), channel_id=1, source_target_pairs={{0,6},{2,8},{4,10},{6,12},{8,14},{10,0},{12,2},{14,4},{1,7},{3,9},... | collective-permute-start | bytes 196616 | tf_op jit(solution)/shard_map/ppermute | solution.py:29
  26.3 30.3 %collective-permute-start.3 = (bf16[1,8,4096]{2,0,1:T(2,128)(2,1)S(1)}, bf16[1,8,4096]{2,0,1:T(2,128)(2,1)}, u32[]{:S(2)}, u32[]{:S(2)}) collective-permute-start(bf16[1,8,4096]{2,0,1:T(2,128)(2,1)S(1)} %get-tuple-element.27), channel_id=1, source_target_pairs={{0,8},{2,10},{4,12},{6,14},{8,0},{10,2},{12,4},{14,6},{1,9},{3,11}... | collective-permute-start | bytes 196616 | tf_op jit(solution)/shard_map/ppermute | solution.py:29
  27.6 31.6 %collective-permute-start.4 = (bf16[1,8,4096]{2,0,1:T(2,128)(2,1)S(1)}, bf16[1,8,4096]{2,0,1:T(2,128)(2,1)}, u32[]{:S(2)}, u32[]{:S(2)}) collective-permute-start(bf16[1,8,4096]{2,0,1:T(2,128)(2,1)S(1)} %get-tuple-element.26), channel_id=1, source_target_pairs={{0,10},{2,12},{4,14},{6,0},{8,2},{10,4},{12,6},{14,8},{1,11},{3,13... | collective-permute-start | bytes 196616 | tf_op jit(solution)/shard_map/ppermute | solution.py:29
  34.0 39.5 %all-to-all-start = ((bf16[8,8,384]{2,0,1:T(8,128)(2,1)}), bf16[8,8,384]{2,0,1:T(8,128)(2,1)S(1)}, u32[]{:S(2)}, u32[]{:S(2)}) async-start(bf16[8,8,384]{2,0,1:T(8,128)(2,1)} %copy.70), calls=%async_computation | async-start | bytes 98304 | tf_op jit(solution)/shard_map/all_to_all | solution.py:94
  37.4 159.7 %all-gather.7.cloned.1.call-start = ((), (), s32[]{:S(2)}) async-start(), calls=%async_computation.2 | async-start | bytes 7077888 | tf_op jit(solution)/shard_map/all_gather | solution.py:126
  44.1 17.6 %collective-permute-start.5 = (bf16[1,8,4096]{2,0,1:T(2,128)(2,1)S(1)}, bf16[1,8,4096]{2,0,1:T(2,128)(2,1)S(1)}, u32[]{:S(2)}, u32[]{:S(2)}) collective-permute-start(bf16[1,8,4096]{2,0,1:T(2,128)(2,1)S(1)} %get-tuple-element.25), channel_id=1, source_target_pairs={{0,12},{2,14},{4,0},{6,2},{8,4},{10,6},{12,8},{14,10},{1,13},{3,15... | collective-permute-start | bytes 196616 | tf_op jit(solution)/shard_map/ppermute | solution.py:29
  47.7 15.3 %collective-permute-start.6 = (bf16[1,8,4096]{2,0,1:T(2,128)(2,1)S(1)}, bf16[1,8,4096]{2,0,1:T(2,128)(2,1)S(1)}, u32[]{:S(2)}, u32[]{:S(2)}) collective-permute-start(bf16[1,8,4096]{2,0,1:T(2,128)(2,1)S(1)} %get-tuple-element.24), channel_id=1, source_target_pairs={{0,14},{2,0},{4,2},{6,4},{8,6},{10,8},{12,10},{14,12},{1,15},{3,1}... | collective-permute-start | bytes 196616 | tf_op jit(solution)/shard_map/ppermute | solution.py:29
  65.1 2.2 slice-start
  65.1 3.6 %slice-start.1 = ((s8[6291456]{0:T(1024)(128)(4,1)}), s8[2097152]{0:T(1024)(128)(4,1)S(1)}, s32[]{:S(2)}) async-start(s8[6291456]{0:T(1024)(128)(4,1)} %bitcast.143), calls=%async_computation.4 | async-start | bytes 4194304
  66.6 3.1 copy-start.2
  66.6 3.1 copy-start.3
  78.5 17.4 %copy-start.1 = (f32[64,1,3,32,64]{4,0,3,2,1:T(8,128)}, f32[64,1,3,32,64]{4,0,3,2,1:T(8,128)S(1)}, u32[]{:S(2)}) copy-start(f32[64,1,3,32,64]{4,0,3,2,1:T(8,128)S(1)} %get-tuple-element.21) | copy-start | bytes 4718596
  99.7 196.8 %all-gather.5.cloned.1.call-start = ((), (), s32[]{:S(2)}) async-start(), calls=%async_computation.1 | async-start | bytes 7077888 | tf_op jit(solution)/shard_map/all_gather | solution.py:123
  206.6 99.6 %copy-start.5 = (f32[32,768]{1,0:T(8,128)S(1)}, f32[32,768]{1,0:T(8,128)}, u32[]{:S(2)}) copy-start(f32[32,768]{1,0:T(8,128)} %param.7) | copy-start | bytes 294916
Sparse Core Ops, SparseCore 0:
  99.8 97.2 all-gather.6
  199.3 97.1 all-gather.4
